TPU v7x, 32 devices: a whole 2x2x4 slice. The times are simulated.
32 devices in a mesh: win: 8 (over z, x), atom: 4 (over y, core).
Axes of the slice: x: 2, y: 2, z: 4, core: 2. Of those that a mesh axis runs over, the one named last changes fastest.
Arguments:
- retarded: bfloat16 [64, 8, 2, 128, 128], P(('win', 'atom')), may hold values from -0.375 to 0.375
- sigma_in: bfloat16 [64, 8, 2, 128, 128], P(('win', 'atom')), may hold values from -6 to 6
- bit_shifts: int32 [3], replicated, may hold values from 0 to 2, as said below
- occupation: float32 [3], replicated, may hold values from 0.3 to 3
- neighbors: int32 [8, 3], replicated, may hold values from 0 to 7, as said below
- coupling: bfloat16 [3, 128, 128], replicated, may hold values from -0.375 to 0.375
Outputs:
- self_energy: bfloat16 [64, 8, 2, 128, 128], P('win', 'atom')
Inputs may be any that keep to these rules, and one draw needn't show every extreme that they name: `bit_shifts`: three different values; among them are 0 and 2, in an order drawn afresh. `neighbors`: column 0 of row b is b itself; the other columns of row b lie within b - 1 to b + 1.
All inputs are finite; a program needn't handle non-finite values.
Results may differ from a plain program's by a relative error of at most 0.007.
Values may be sent and summed in bfloat16 or wider, within the bound.
No kernel may reach another device: no remote copies, remote signals or barrier semaphores. Data moves between devices by JAX's collectives and lax.ppermute only.
A program may use at most 128 MiB of HBM per device.

v0:
```python
import jax
import jax.numpy as jnp
from jax import lax
from jax.sharding import PartitionSpec as P


def partner(value, axis, distance):
    mask = 2**distance
    pairs = [(source, source ^ mask) for source in range(lax.axis_size(axis))]
    return lax.ppermute(value, axis, pairs)


def complex_product(left, right, form):
    real_part = jnp.einsum(
        form, left[:, :, 0], right[:, :, 0], preferred_element_type=jnp.float32
    ) - jnp.einsum(form, left[:, :, 1], right[:, :, 1], preferred_element_type=jnp.float32)
    imag_part = jnp.einsum(
        form, left[:, :, 0], right[:, :, 1], preferred_element_type=jnp.float32
    ) + jnp.einsum(form, left[:, :, 1], right[:, :, 0], preferred_element_type=jnp.float32)
    return jnp.stack([real_part, imag_part], axis=2).astype(jnp.bfloat16)


def partner_sum(lesser, bit_shifts, occupation):
    bit_count = lax.axis_size("win").bit_length() - 1
    summed = jnp.zeros(lesser.shape, jnp.float32)
    for bit_number in range(bit_count):
        weight = jnp.sum(jnp.where(bit_shifts == bit_number, occupation, 0.0))
        arrived = partner(lesser, "win", bit_number)
        summed = summed + weight * arrived.astype(jnp.float32)
    return summed.astype(jnp.bfloat16)


def couple(source, indices, coupling):
    directions = coupling.shape[0]
    picks = [jnp.take(source, indices[:, direction], axis=1) for direction in range(directions)]
    result = jnp.zeros(picks[0].shape, jnp.float32)
    for direction in range(directions):
        bent = jnp.einsum(
            "ij,erxjk->erxik",
            coupling[direction],
            picks[direction],
            preferred_element_type=jnp.float32,
        ).astype(jnp.bfloat16)
        result = result + jnp.einsum(
            "erxij,kj->erxik", bent, coupling[direction], preferred_element_type=jnp.float32
        )
    return result.astype(jnp.bfloat16)


def on_device(retarded, sigma_in, bit_shifts, occupation, neighbors, coupling):
    product = complex_product(retarded, sigma_in, "ebij,ebjk->ebik")
    lesser = complex_product(product, retarded, "ebij,ebkj->ebik")
    partners = partner_sum(lesser, bit_shifts, occupation)
    energy_side = couple(partners, neighbors, coupling)
    return lax.all_to_all(energy_side, "atom", split_axis=1, concat_axis=0, tiled=True)


def solution(mesh):
    return jax.shard_map(
        on_device,
        mesh=mesh,
        in_specs=(
            P(("win", "atom"), None, None, None, None),
            P(("win", "atom"), None, None, None, None),
            P(),
            P(),
            P(),
            P(),
        ),
        out_specs=P("win", "atom", None, None, None),
        check_vma=False,
    )
```

profile of v0, /device:TPU:0, one launch (start us, length us, event | category | flops | bytes accessed | tf_op | source)
XLA Modules:
  0.0 89.7 jit_solution(15645201465588671409)
XLA Ops:
  0.0 0.0 copy-start
  0.0 0.0 copy-start.1
  0.0 1.6 %fusion.17 = f32[2,8,128,128]{3,2,1,0:T(8,128)S(1)} fusion(bf16[2,8,2,128,128]{4,3,2,1,0:T(8,128)(2,1)} %param.9, bf16[2,8,2,128,128]{4,3,2,1,0:T(8,128)(2,1)} %param.8), kind=kOutput, calls=%fused_computation.30 | convolution fusion | flops 67108864 | bytes 2097152 | tf_op jit(solution)/shard_map/ebij,ebjk->ebik/dot_general | solution.py:17
  1.7 0.0 copy-done
  1.7 0.2 copy-done.1
  1.9 0.3 fusion.26
  2.2 0.3 fusion.5
  2.5 0.5 fusion.20
  2.9 0.5 fusion.30
  3.4 0.3 fusion.6
  3.7 0.5 fusion.9
  4.2 0.0 copy-start.3
  4.2 0.0 copy-start.4
  4.2 0.0 copy-start.5
  4.3 0.5 fusion.10
  4.7 0.1 pad_maximum_fusion
  4.8 4.1 %collective-permute-start.2 = (bf16[2,8,2,128,128]{4,3,1,0,2:T(8,128)(2,1)S(1)}, bf16[2,8,2,128,128]{4,3,1,0,2:T(8,128)(2,1)S(1)}, u32[]{:S(2)}, u32[]{:S(2)}) collective-permute-start(bf16[2,8,2,128,128]{4,3,1,0,2:T(8,128)(2,1)S(1)} %pad_maximum_fusion), channel_id=1, source_target_pairs={{0,16},{4,20},{8,24},{12,28},{16,0},{20,4},{24,8},{28,12},{1,17},{... | collective-permute-start | bytes 3145736 | tf_op jit(solution)/shard_map/ppermute | solution.py:10
  9.0 1.6 %collective-permute-start.1 = (bf16[2,8,2,128,128]{4,3,1,0,2:T(8,128)(2,1)S(1)}, bf16[2,8,2,128,128]{4,3,1,0,2:T(8,128)(2,1)S(1)}, u32[]{:S(2)}, u32[]{:S(2)}) collective-permute-start(bf16[2,8,2,128,128]{4,3,1,0,2:T(8,128)(2,1)S(1)} %pad_maximum_fusion), channel_id=1, source_target_pairs={{0,8},{4,12},{8,0},{12,4},{16,24},{20,28},{24,16},{28,20},{1,9},{5... | collective-permute-start | bytes 3145736 | tf_op jit(solution)/shard_map/ppermute | solution.py:10
  10.5 1.5 %collective-permute-start = (bf16[2,8,2,128,128]{4,3,1,0,2:T(8,128)(2,1)S(1)}, bf16[2,8,2,128,128]{4,3,1,0,2:T(8,128)(2,1)S(1)}, u32[]{:S(2)}, u32[]{:S(2)}) collective-permute-start(bf16[2,8,2,128,128]{4,3,1,0,2:T(8,128)(2,1)S(1)} %pad_maximum_fusion), channel_id=1, source_target_pairs={{0,4},{4,0},{8,12},{12,8},{16,20},{20,16},{24,28},{28,24},{1,5},{5... | collective-permute-start | bytes 3145736 | tf_op jit(solution)/shard_map/ppermute | solution.py:10
  12.0 0.0 copy-done.3
  12.1 0.0 copy-done.4
  12.1 0.0 copy-done.5
  12.1 0.6 fusion.57
  12.8 41.9 %collective-permute-done.2 = bf16[2,8,2,128,128]{4,3,1,0,2:T(8,128)(2,1)S(1)} collective-permute-done((bf16[2,8,2,128,128]{4,3,1,0,2:T(8,128)(2,1)S(1)}, bf16[2,8,2,128,128]{4,3,1,0,2:T(8,128)(2,1)S(1)}, u32[]{:S(2)}, u32[]{:S(2)}) %collective-permute-start.2) | collective-permute-done | bytes 1048608 | tf_op jit(solution)/shard_map/ppermute | solution.py:10
  54.7 0.2 collective-permute-done.1
  54.9 0.0 collective-permute-done
  54.9 2.5 %add_convert_fusion.1 = bf16[2,8,2,128,128]{4,3,1,0,2:T(8,128)(2,1)S(1)} fusion(bf16[2,8,2,128,128]{4,3,1,0,2:T(8,128)(2,1)S(1)} %collective-permute-done.2, bf16[2,8,2,128,128]{4,3,1,0,2:T(8,128)(2,1)S(1)} %collective-permute-done.1, bf16[2,8,2,128,128]{4,3,1,0,2:T(8,128)(2,1)S(1)} %collective-permute-done, f32[]{:T(128)} %get-tuple-element.7, ...), kind=kLoop, calls=%fused_computation.4 | loop fusion | flops 4718592 | bytes 4194316 | tf_op jit(solution)/shard_map/convert_element_type | solution.py:30
  57.4 0.7 gather_fusion.2
  58.1 0.7 gather_fusion.1
  58.9 1.7 %gather_fusion = bf16[8,2,2,128,128]{4,3,1,2,0:T(8,128)(2,1)} fusion(bf16[2,8,2,128,128]{4,3,1,0,2:T(8,128)(2,1)S(1)} %add_convert_fusion.1, s32[1024]{0:T(1024)S(1)} %pad_clamp_fusion.2), kind=kCustom, calls=%fused_computation.clone | custom fusion | bytes 2097184 | tf_op jit(solution)/shard_map/jit(_take)/gather | solution.py:35
  60.5 0.0 copy-start.2
  60.6 1.2 %select_bitcast_fusion = (bf16[2,8,2,128,128]{4,3,0,2,1:T(8,128)(2,1)S(1)}, bf16[2,8,2,128,128]{4,3,0,2,1:T(8,128)(2,1)}) fusion(bf16[8,2,2,128,128]{4,3,1,2,0:T(8,128)(2,1)S(1)} %gather_fusion.2, pred[8]{0:T(512)(128)(4,1)S(1)} %get-tuple-element.9, bf16[8,2,2,128,128]{4,3,1,2,0:T(8,128)(2,1)S(1)} %gather_fusion.1, pred[8]{0:T(512)(128)(4,1)S(1)} %get-tuple-element.17), kind=kLoop, calls=%fused_computation.27 | loop fusion | flops 1048576 | bytes 4194320 | tf_op jit(solution)/shard_map/jit(_take)/select_n | solution.py:35
  61.8 0.0 copy-done.2
  61.8 1.9 %fusion.3 = f32[2,8,2,128,128]{4,3,2,1,0:T(8,128)S(1)} fusion(bf16[2,8,2,128,128]{4,3,0,2,1:T(8,128)(2,1)} %get-tuple-element.20, bf16[3,128,128]{2,1,0:T(8,128)(2,1)S(1)} %copy-done.2), kind=kOutput, calls=%fused_computation.11 | convolution fusion | flops 268959744 | bytes 3211264 | tf_op jit(solution)/shard_map/erxij,kj->erxik/dot_general | solution.py:44
  63.7 3.3 %fusion.1 = f32[2,8,2,128,128]{4,3,2,1,0:T(8,128)} fusion(bf16[3,128,128]{2,1,0:T(8,128)(2,1)S(1)} %copy-done.2, bf16[8,2,2,128,128]{4,3,1,2,0:T(8,128)(2,1)} %gather_fusion, pred[8]{0:T(512)(128)(4,1)S(1)} %get-tuple-element.15), kind=kOutput, calls=%fused_computation.9 | convolution fusion | flops 269484032 | bytes 3211776 | tf_op jit(solution)/shard_map/erxij,kj->erxik/dot_general | solution.py:44
  67.0 3.3 %add_convert_fusion = bf16[2,8,2,128,128]{4,3,2,1,0:T(8,128)(2,1)} fusion(f32[2,8,2,128,128]{4,3,2,1,0:T(8,128)} %fusion.1, f32[2,8,2,128,128]{4,3,2,1,0:T(8,128)S(1)} %fusion.3, bf16[2,8,2,128,128]{4,3,0,2,1:T(8,128)(2,1)S(1)} %get-tuple-element.19, bf16[3,128,128]{2,1,0:T(8,128)(2,1)S(1)} %copy-done.2), kind=kOutput, calls=%fused_computation.3 | convolution fusion | flops 270532608 | bytes 6356992 | tf_op jit(solution)/shard_map/erxij,kj->erxik/dot_general | solution.py:44
  70.3 1.3 %copy.16 = bf16[2,8,2,128,128]{4,3,2,0,1:T(8,128)(2,1)S(1)} copy(bf16[2,8,2,128,128]{4,3,2,1,0:T(8,128)(2,1)} %add_convert_fusion) | data formatting | bytes 2097152 | tf_op jit(solution)/shard_map/convert_element_type | solution.py:47
  71.6 17.1 %all_to_all.18 = bf16[2,8,2,128,128]{4,3,2,0,1:T(8,128)(2,1)S(1)} all-to-all(bf16[2,8,2,128,128]{4,3,2,0,1:T(8,128)(2,1)S(1)} %copy.16), channel_id=1, replica_groups=mesh['win'=8,'atom'=4] {'atom'}, dimensions={1} | all-to-all | bytes 2097152 | tf_op jit(solution)/shard_map/all_to_all | solution.py:55
  88.7 1.0 %copy.17 = bf16[4,2,2,2,128,128]{5,4,3,2,1,0:T(8,128)(2,1)} copy(bf16[4,2,2,2,128,128]{5,4,3,1,2,0:T(8,128)(2,1)S(1)} %bitcast.102) | data formatting | bytes 2097152 | tf_op jit(solution)/shard_map/all_to_all | solution.py:55
  (4 shorter events, 0.0 us)
Async XLA Ops:
  0.0 1.7 %copy-start = (bf16[2,8,2,128,128]{4,3,2,1,0:T(8,128)(2,1)S(1)}, bf16[2,8,2,128,128]{4,3,2,1,0:T(8,128)(2,1)}, u32[]{:S(2)}) copy-start(bf16[2,8,2,128,128]{4,3,2,1,0:T(8,128)(2,1)} %param.8) | copy-start | bytes 3145732
  0.0 1.9 %copy-start.1 = (bf16[2,8,2,128,128]{4,3,2,1,0:T(8,128)(2,1)S(1)}, bf16[2,8,2,128,128]{4,3,2,1,0:T(8,128)(2,1)}, u32[]{:S(2)}) copy-start(bf16[2,8,2,128,128]{4,3,2,1,0:T(8,128)(2,1)} %param.9) | copy-start | bytes 3145732
  4.2 7.8 %copy-start.3 = (s32[8,3]{0,1:T(4,128)S(1)}, s32[8,3]{0,1:T(4,128)}, u32[]{:S(2)}) copy-start(s32[8,3]{0,1:T(4,128)} %param.12) | copy-start | bytes 292
  4.2 7.9 %copy-start.4 = (f32[3]{0:T(128)S(1)}, f32[3]{0:T(128)}, u32[]{:S(2)}) copy-start(f32[3]{0:T(128)} %param.11) | copy-start | bytes 40
  4.2 7.9 %copy-start.5 = (s32[3]{0:T(128)S(1)}, s32[3]{0:T(128)}, u32[]{:S(2)}) copy-start(s32[3]{0:T(128)} %param.10) | copy-start | bytes 40
  4.8 49.8 %collective-permute-start.2 = (bf16[2,8,2,128,128]{4,3,1,0,2:T(8,128)(2,1)S(1)}, bf16[2,8,2,128,128]{4,3,1,0,2:T(8,128)(2,1)S(1)}, u32[]{:S(2)}, u32[]{:S(2)}) collective-permute-start(bf16[2,8,2,128,128]{4,3,1,0,2:T(8,128)(2,1)S(1)} %pad_maximum_fusion), channel_id=1, source_target_pairs={{0,16},{4,20},{8,24},{12,28},{16,0},{20,4},{24,8},{28,12},{1,17},{... | collective-permute-start | bytes 3145736 | tf_op jit(solution)/shard_map/ppermute | solution.py:10
  9.0 45.9 %collective-permute-start.1 = (bf16[2,8,2,128,128]{4,3,1,0,2:T(8,128)(2,1)S(1)}, bf16[2,8,2,128,128]{4,3,1,0,2:T(8,128)(2,1)S(1)}, u32[]{:S(2)}, u32[]{:S(2)}) collective-permute-start(bf16[2,8,2,128,128]{4,3,1,0,2:T(8,128)(2,1)S(1)} %pad_maximum_fusion), channel_id=1, source_target_pairs={{0,8},{4,12},{8,0},{12,4},{16,24},{20,28},{24,16},{28,20},{1,9},{5... | collective-permute-start | bytes 3145736 | tf_op jit(solution)/shard_map/ppermute | solution.py:10
  10.5 44.4 %collective-permute-start = (bf16[2,8,2,128,128]{4,3,1,0,2:T(8,128)(2,1)S(1)}, bf16[2,8,2,128,128]{4,3,1,0,2:T(8,128)(2,1)S(1)}, u32[]{:S(2)}, u32[]{:S(2)}) collective-permute-start(bf16[2,8,2,128,128]{4,3,1,0,2:T(8,128)(2,1)S(1)} %pad_maximum_fusion), channel_id=1, source_target_pairs={{0,4},{4,0},{8,12},{12,8},{16,20},{20,16},{24,28},{28,24},{1,5},{5... | collective-permute-start | bytes 3145736 | tf_op jit(solution)/shard_map/ppermute | solution.py:10
  60.5 1.2 %copy-start.2 = (bf16[3,128,128]{2,1,0:T(8,128)(2,1)S(1)}, bf16[3,128,128]{2,1,0:T(8,128)(2,1)}, u32[]{:S(2)}) copy-start(bf16[3,128,128]{2,1,0:T(8,128)(2,1)} %param.13) | copy-start | bytes 294916
where the time goes:
time: 90 us; the launch traced here: 89.7 us
  waiting for transfers between devices  42.1 us (47%)
  blocking collectives  17.1 us (19%)
  matrix products  13 us (14%)
  starting transfers between devices  7.2 us (8%)
  local copies, waits for them, and re-layouts  5.71 us (6%)
  other arithmetic  4.47 us (5%)
    ppermute x3, waiting for transfers between devices, partner(): return lax.ppermute(value, axis, pairs)  42.1 us
    all_to_all x1, blocking collectives, on_device(): lax.all_to_all(energy_side, 'atom', split_axis=1, concat_axis=0, tiled=True)  17.1 us
    dot_general x3, matrix products, couple(): jnp.einsum('erxij,kj->erxik', bent, coupling[direction], preferred_elemen...  8.53 us
    ppermute x3, starting transfers between devices, partner(): return lax.ppermute(value, axis, pairs)  7.2 us
    gather x3, local copies, waits for them, and re-layouts, couple(): jnp.take(source, indices[:, direction], axis=1)  3.15 us
    convert_element_type x1, other arithmetic, partner_sum(): return summed.astype(jnp.bfloat16)  2.49 us
    dot_general x2, matrix products, complex_product(): jnp.einsum(form, left[:, :, 0], right[:, :, 1], preferred_element_type=jn...  2.13 us
  transfers between devices with their start and end apart: 3, of which 2 were waited for; matrix products, arithmetic and copies ran while one was open for 1% of the time, Pallas kernels for 0%

commit v1 on v0

--- a/solution.py
+++ b/solution.py
@@ -2,6 +2,13 @@
 import jax.numpy as jnp
 from jax import lax
 from jax.sharding import PartitionSpec as P
+
+
+def swap_blocks(block, axis, split, join):
+    devices = lax.axis_size(axis)
+    shards = jnp.stack(jnp.split(block, devices, axis=split), axis=0)
+    shards = lax.all_to_all(shards, axis, split_axis=0, concat_axis=0)
+    return jnp.concatenate(shards, axis=join)
 
 
 def partner(value, axis, distance):
@@ -52,7 +59,7 @@
     lesser = complex_product(product, retarded, "ebij,ebkj->ebik")
     partners = partner_sum(lesser, bit_shifts, occupation)
     energy_side = couple(partners, neighbors, coupling)
-    return lax.all_to_all(energy_side, "atom", split_axis=1, concat_axis=0, tiled=True)
+    return swap_blocks(energy_side, "atom", 1, 0)
 
 
 def solution(mesh):

time: 90 us -> 90 us (level)
    convert_element_type x1 -> x0, local copies, waits for them, and re-layouts: 1.29 us -> none  [couple(): return result.astype(jnp.bfloat16)]
    another operation x0 -> x1, local copies, waits for them, and re-layouts: none -> 1.26 us  [swap_blocks(): shards = jnp.stack(jnp.split(block, devices, axis=split), axis=0)]
    all_to_all x1 -> x0, local copies, waits for them, and re-layouts: 1.04 us -> none  [on_device(): lax.all_to_all(energy_side, 'atom', split_axis=1, concat_axis=0, tiled=True)]
    unnamed x12 -> x13, local copies, waits for them, and re-layouts: 0.23 us -> 1.2 us
where the time goes in v1:
time: 90 us; the launch traced here: 89.7 us
  waiting for transfers between devices  42.2 us (47%)
  blocking collectives  17.1 us (19%)
  matrix products  13 us (14%)
  starting transfers between devices  7.2 us (8%)
  local copies, waits for them, and re-layouts  5.6 us (6%)
  other arithmetic  4.53 us (5%)
    ppermute x3, waiting for transfers between devices, partner(): return lax.ppermute(value, axis, pairs)  42.2 us
    all_to_all x1, blocking collectives, swap_blocks(): shards = lax.all_to_all(shards, axis, split_axis=0, concat_axis=0)  17.1 us
    dot_general x3, matrix products, couple(): jnp.einsum('erxij,kj->erxik', bent, coupling[direction], preferred_elemen...  8.52 us
    ppermute x3, starting transfers between devices, partner(): return lax.ppermute(value, axis, pairs)  7.2 us
    gather x3, local copies, waits for them, and re-layouts, couple(): jnp.take(source, indices[:, direction], axis=1)  3.15 us
    convert_element_type x1, other arithmetic, partner_sum(): return summed.astype(jnp.bfloat16)  2.44 us
    dot_general x2, matrix products, complex_product(): jnp.einsum(form, left[:, :, 0], right[:, :, 1], preferred_element_type=jn...  2.13 us
  transfers between devices with their start and end apart: 3, of which 2 were waited for; matrix products, arithmetic and copies ran while one was open for 1% of the time, Pallas kernels for 0%

profile of v1, /device:TPU:0, one launch (start us, length us, event | category | flops | bytes accessed | tf_op | source)
XLA Modules:
  0.0 89.7 jit_solution(13768394453677847581)
XLA Ops:
  0.0 0.0 copy-start
  0.0 0.0 copy-start.1
  0.0 1.6 %fusion.17 = f32[2,8,128,128]{3,2,1,0:T(8,128)S(1)} fusion(bf16[2,8,2,128,128]{4,3,2,1,0:T(8,128)(2,1)} %param.9, bf16[2,8,2,128,128]{4,3,2,1,0:T(8,128)(2,1)} %param.8), kind=kOutput, calls=%fused_computation.31 | convolution fusion | flops 67108864 | bytes 2097152 | tf_op jit(solution)/shard_map/ebij,ebjk->ebik/dot_general | solution.py:24
  1.7 0.0 copy-done
  1.7 0.2 copy-done.1
  1.9 0.3 fusion.26
  2.2 0.3 fusion.5
  2.5 0.5 fusion.20
  2.9 0.5 fusion.30
  3.4 0.3 fusion.6
  3.7 0.5 fusion.9
  4.2 0.0 copy-start.3
  4.2 0.0 copy-start.4
  4.2 0.0 copy-start.5
  4.3 0.5 fusion.10
  4.7 0.1 pad_maximum_fusion
  4.8 4.1 %collective-permute-start.2 = (bf16[2,8,2,128,128]{4,3,1,0,2:T(8,128)(2,1)S(1)}, bf16[2,8,2,128,128]{4,3,1,0,2:T(8,128)(2,1)S(1)}, u32[]{:S(2)}, u32[]{:S(2)}) collective-permute-start(bf16[2,8,2,128,128]{4,3,1,0,2:T(8,128)(2,1)S(1)} %pad_maximum_fusion), channel_id=1, source_target_pairs={{0,16},{4,20},{8,24},{12,28},{16,0},{20,4},{24,8},{28,12},{1,17},{... | collective-permute-start | bytes 3145736 | tf_op jit(solution)/shard_map/ppermute | solution.py:17
  9.0 1.6 %collective-permute-start.1 = (bf16[2,8,2,128,128]{4,3,1,0,2:T(8,128)(2,1)S(1)}, bf16[2,8,2,128,128]{4,3,1,0,2:T(8,128)(2,1)S(1)}, u32[]{:S(2)}, u32[]{:S(2)}) collective-permute-start(bf16[2,8,2,128,128]{4,3,1,0,2:T(8,128)(2,1)S(1)} %pad_maximum_fusion), channel_id=1, source_target_pairs={{0,8},{4,12},{8,0},{12,4},{16,24},{20,28},{24,16},{28,20},{1,9},{5... | collective-permute-start | bytes 3145736 | tf_op jit(solution)/shard_map/ppermute | solution.py:17
  10.5 1.5 %collective-permute-start = (bf16[2,8,2,128,128]{4,3,1,0,2:T(8,128)(2,1)S(1)}, bf16[2,8,2,128,128]{4,3,1,0,2:T(8,128)(2,1)S(1)}, u32[]{:S(2)}, u32[]{:S(2)}) collective-permute-start(bf16[2,8,2,128,128]{4,3,1,0,2:T(8,128)(2,1)S(1)} %pad_maximum_fusion), channel_id=1, source_target_pairs={{0,4},{4,0},{8,12},{12,8},{16,20},{20,16},{24,28},{28,24},{1,5},{5... | collective-permute-start | bytes 3145736 | tf_op jit(solution)/shard_map/ppermute | solution.py:17
  12.0 0.0 copy-done.3
  12.1 0.0 copy-done.4
  12.1 0.0 copy-done.5
  12.1 0.6 fusion.57
  12.7 42.0 %collective-permute-done.2 = bf16[2,8,2,128,128]{4,3,1,0,2:T(8,128)(2,1)S(1)} collective-permute-done((bf16[2,8,2,128,128]{4,3,1,0,2:T(8,128)(2,1)S(1)}, bf16[2,8,2,128,128]{4,3,1,0,2:T(8,128)(2,1)S(1)}, u32[]{:S(2)}, u32[]{:S(2)}) %collective-permute-start.2) | collective-permute-done | bytes 1048608 | tf_op jit(solution)/shard_map/ppermute | solution.py:17
  54.7 0.2 collective-permute-done.1
  54.9 0.0 collective-permute-done
  54.9 2.4 %add_convert_fusion.1 = bf16[2,8,2,128,128]{4,3,1,0,2:T(8,128)(2,1)S(1)} fusion(bf16[2,8,2,128,128]{4,3,1,0,2:T(8,128)(2,1)S(1)} %collective-permute-done.2, bf16[2,8,2,128,128]{4,3,1,0,2:T(8,128)(2,1)S(1)} %collective-permute-done.1, bf16[2,8,2,128,128]{4,3,1,0,2:T(8,128)(2,1)S(1)} %collective-permute-done, f32[]{:T(128)} %get-tuple-element.7, ...), kind=kLoop, calls=%fused_computation.4 | loop fusion | flops 4718592 | bytes 4194316 | tf_op jit(solution)/shard_map/convert_element_type | solution.py:37
  57.3 0.7 gather_fusion.2
  58.1 0.7 gather_fusion.1
  58.8 1.7 %gather_fusion = bf16[8,2,2,128,128]{4,3,1,2,0:T(8,128)(2,1)} fusion(bf16[2,8,2,128,128]{4,3,1,0,2:T(8,128)(2,1)S(1)} %add_convert_fusion.1, s32[1024]{0:T(1024)S(1)} %pad_clamp_fusion.2), kind=kCustom, calls=%fused_computation.clone | custom fusion | bytes 2097184 | tf_op jit(solution)/shard_map/jit(_take)/gather | solution.py:42
  60.5 0.0 copy-start.2
  60.5 1.2 %select_bitcast_fusion = (bf16[2,8,2,128,128]{4,3,0,2,1:T(8,128)(2,1)S(1)}, bf16[2,8,2,128,128]{4,3,0,2,1:T(8,128)(2,1)}) fusion(bf16[8,2,2,128,128]{4,3,1,2,0:T(8,128)(2,1)S(1)} %gather_fusion.2, pred[8]{0:T(512)(128)(4,1)S(1)} %get-tuple-element.9, bf16[8,2,2,128,128]{4,3,1,2,0:T(8,128)(2,1)S(1)} %gather_fusion.1, pred[8]{0:T(512)(128)(4,1)S(1)} %get-tuple-element.21), kind=kLoop, calls=%fused_computation.28 | loop fusion | flops 1048576 | bytes 4194320 | tf_op jit(solution)/shard_map/jit(_take)/select_n | solution.py:42
  61.7 0.0 copy-done.2
  61.7 1.9 %fusion.3 = f32[2,8,2,128,128]{4,3,2,1,0:T(8,128)S(1)} fusion(bf16[2,8,2,128,128]{4,3,0,2,1:T(8,128)(2,1)} %get-tuple-element.24, bf16[3,128,128]{2,1,0:T(8,128)(2,1)S(1)} %copy-done.2), kind=kOutput, calls=%fused_computation.11 | convolution fusion | flops 268959744 | bytes 3211264 | tf_op jit(solution)/shard_map/erxij,kj->erxik/dot_general | solution.py:51
  63.6 3.3 %fusion.1 = f32[2,8,2,128,128]{4,3,2,1,0:T(8,128)} fusion(bf16[3,128,128]{2,1,0:T(8,128)(2,1)S(1)} %copy-done.2, bf16[8,2,2,128,128]{4,3,1,2,0:T(8,128)(2,1)} %gather_fusion, pred[8]{0:T(512)(128)(4,1)S(1)} %get-tuple-element.19), kind=kOutput, calls=%fused_computation.9 | convolution fusion | flops 269484032 | bytes 3211776 | tf_op jit(solution)/shard_map/erxij,kj->erxik/dot_general | solution.py:51
  67.0 3.3 %add_convert_fusion = bf16[2,8,2,128,128]{4,3,2,1,0:T(8,128)(2,1)} fusion(f32[2,8,2,128,128]{4,3,2,1,0:T(8,128)} %fusion.1, f32[2,8,2,128,128]{4,3,2,1,0:T(8,128)S(1)} %fusion.3, bf16[2,8,2,128,128]{4,3,0,2,1:T(8,128)(2,1)S(1)} %get-tuple-element.23, bf16[3,128,128]{2,1,0:T(8,128)(2,1)S(1)} %copy-done.2), kind=kOutput, calls=%fused_computation.3 | convolution fusion | flops 270532608 | bytes 6356992 | tf_op jit(solution)/shard_map/erxij,kj->erxik/dot_general | solution.py:51
  70.3 1.3 %slice_bitcast_fusion.3 = (bf16[1,2,2,2,128,128]{5,4,3,2,1,0:T(8,128)(2,1)S(1)}, bf16[1,2,2,2,128,128]{5,4,3,2,1,0:T(8,128)(2,1)S(1)}, bf16[1,2,2,2,128,128]{5,4...) fusion(bf16[2,8,2,128,128]{4,3,2,1,0:T(8,128)(2,1)} %add_convert_fusion), kind=kLoop, calls=%fused_computation.62 | loop fusion | bytes 2097152 | tf_op jit(solution)/shard_map/stack | solution.py:9
  71.5 0.1 pad_maximum_fusion.1
  71.7 17.1 %all_to_all.5 = bf16[4,2,2,2,128,128]{5,4,3,2,1,0:T(8,128)(2,1)S(1)} all-to-all(bf16[4,2,2,2,128,128]{5,4,3,2,1,0:T(8,128)(2,1)S(1)} %pad_maximum_fusion.1), channel_id=1, replica_groups=mesh['win'=8,'atom'=4] {'atom'}, dimensions={0} | all-to-all | bytes 2097152 | tf_op jit(solution)/shard_map/all_to_all | solution.py:10
  88.7 1.0 %copy.31 = bf16[8,2,2,128,128]{4,3,2,1,0:T(8,128)(2,1)} copy(bf16[8,2,2,128,128]{4,3,2,1,0:T(8,128)(2,1)S(1)} %bitcast.107) | data formatting | bytes 2097152
  (4 shorter events, 0.0 us)
Async XLA Ops:
  0.0 1.7 %copy-start = (bf16[2,8,2,128,128]{4,3,2,1,0:T(8,128)(2,1)S(1)}, bf16[2,8,2,128,128]{4,3,2,1,0:T(8,128)(2,1)}, u32[]{:S(2)}) copy-start(bf16[2,8,2,128,128]{4,3,2,1,0:T(8,128)(2,1)} %param.8) | copy-start | bytes 3145732
  0.0 1.9 %copy-start.1 = (bf16[2,8,2,128,128]{4,3,2,1,0:T(8,128)(2,1)S(1)}, bf16[2,8,2,128,128]{4,3,2,1,0:T(8,128)(2,1)}, u32[]{:S(2)}) copy-start(bf16[2,8,2,128,128]{4,3,2,1,0:T(8,128)(2,1)} %param.9) | copy-start | bytes 3145732
  4.2 7.8 %copy-start.3 = (s32[8,3]{0,1:T(4,128)S(1)}, s32[8,3]{0,1:T(4,128)}, u32[]{:S(2)}) copy-start(s32[8,3]{0,1:T(4,128)} %param.12) | copy-start | bytes 292
  4.2 7.9 %copy-start.4 = (f32[3]{0:T(128)S(1)}, f32[3]{0:T(128)}, u32[]{:S(2)}) copy-start(f32[3]{0:T(128)} %param.11) | copy-start | bytes 40
  4.2 7.9 %copy-start.5 = (s32[3]{0:T(128)S(1)}, s32[3]{0:T(128)}, u32[]{:S(2)}) copy-start(s32[3]{0:T(128)} %param.10) | copy-start | bytes 40
  4.8 49.8 %collective-permute-start.2 = (bf16[2,8,2,128,128]{4,3,1,0,2:T(8,128)(2,1)S(1)}, bf16[2,8,2,128,128]{4,3,1,0,2:T(8,128)(2,1)S(1)}, u32[]{:S(2)}, u32[]{:S(2)}) collective-permute-start(bf16[2,8,2,128,128]{4,3,1,0,2:T(8,128)(2,1)S(1)} %pad_maximum_fusion), channel_id=1, source_target_pairs={{0,16},{4,20},{8,24},{12,28},{16,0},{20,4},{24,8},{28,12},{1,17},{... | collective-permute-start | bytes 3145736 | tf_op jit(solution)/shard_map/ppermute | solution.py:17
  9.0 45.9 %collective-permute-start.1 = (bf16[2,8,2,128,128]{4,3,1,0,2:T(8,128)(2,1)S(1)}, bf16[2,8,2,128,128]{4,3,1,0,2:T(8,128)(2,1)S(1)}, u32[]{:S(2)}, u32[]{:S(2)}) collective-permute-start(bf16[2,8,2,128,128]{4,3,1,0,2:T(8,128)(2,1)S(1)} %pad_maximum_fusion), channel_id=1, source_target_pairs={{0,8},{4,12},{8,0},{12,4},{16,24},{20,28},{24,16},{28,20},{1,9},{5... | collective-permute-start | bytes 3145736 | tf_op jit(solution)/shard_map/ppermute | solution.py:17
  10.5 44.4 %collective-permute-start = (bf16[2,8,2,128,128]{4,3,1,0,2:T(8,128)(2,1)S(1)}, bf16[2,8,2,128,128]{4,3,1,0,2:T(8,128)(2,1)S(1)}, u32[]{:S(2)}, u32[]{:S(2)}) collective-permute-start(bf16[2,8,2,128,128]{4,3,1,0,2:T(8,128)(2,1)S(1)} %pad_maximum_fusion), channel_id=1, source_target_pairs={{0,4},{4,0},{8,12},{12,8},{16,20},{20,16},{24,28},{28,24},{1,5},{5... | collective-permute-start | bytes 3145736 | tf_op jit(solution)/shard_map/ppermute | solution.py:17
  60.5 1.2 %copy-start.2 = (bf16[3,128,128]{2,1,0:T(8,128)(2,1)S(1)}, bf16[3,128,128]{2,1,0:T(8,128)(2,1)}, u32[]{:S(2)}) copy-start(bf16[3,128,128]{2,1,0:T(8,128)(2,1)} %param.13) | copy-start | bytes 294916
